TPU v7x, 32 devices: a whole 2x2x4 slice. The times are simulated.
32 devices in a mesh: ma: 4 (over y, x), freq: 8 (over z, core).
Axes of the slice: x: 2, y: 2, z: 4, core: 2. Of those that a mesh axis runs over, the one named last changes fastest.
Arguments:
- m_table: int32 [8], P('ma'), may hold values from 0 to 1023, as said below
- retained_modes: int32 [8], P('ma'), may hold values from 128 to 512, as said below
- cycle_ids: int32 [32], P('ma'), may hold values from 1 to 2047, as said below
- kl_coeffs: bfloat16 [8, 4, 512], P('ma', None, 'freq'), may hold values from -6 to 6
- kl_vectors: bfloat16 [8, 512, 32, 512], P('ma', 'freq'), may hold values from -0.375 to 0.375
- beam_matrix: bfloat16 [8, 32, 1024, 512], P('ma', 'freq'), may hold values from -0.00390625 to 0.00390625
Outputs:
- sky_maps: float32 [32, 2, 32, 2048], P('ma', None, 'freq')
Inputs may be any that keep to these rules, and one draw needn't show every extreme that they name: `m_table`: all distinct; slots 2 q and 2 q + 1 hold two numbers that sum to 1023. `retained_modes`: some slot keeps all 512 modes. `cycle_ids`: all distinct.
All inputs are finite; a program needn't handle non-finite values.
Results may differ from a plain program's by a relative error of at most 0.01.
Values may be sent and summed in bfloat16 or wider, within the bound.
A program may use at most 64 MiB of HBM per device.

v0:
```python
import math

import jax
import jax.numpy as jnp
from jax import lax
from jax.sharding import PartitionSpec as P

NPHI = 2048
L = 1024
NSIDE = 512


def cycle_angles(cycle_numbers):
    cycle_float = cycle_numbers.astype(jnp.float32)
    nside_float = float(NSIDE)
    from_pole = jnp.minimum(cycle_float, 4.0 * nside_float - cycle_float)
    hemisphere = jnp.where(cycle_float <= 2.0 * nside_float, 1.0, -1.0)
    polar_part = from_pole * from_pole / (3.0 * nside_float * nside_float)
    colatitude_cosine = 1.0 - polar_part
    polar_sin = from_pole / (math.sqrt(3.0) * nside_float) * jnp.sqrt(2.0 - polar_part)
    latitude_cosine = 4.0 / 3.0 - 2.0 * from_pole / (3.0 * nside_float)
    latitude_sine = jnp.sqrt(jnp.maximum(1.0 - latitude_cosine * latitude_cosine, 0.25))
    in_cap = from_pole < nside_float
    cos_theta = hemisphere * jnp.where(in_cap, colatitude_cosine, latitude_cosine)
    sin_theta = jnp.where(in_cap, polar_sin, latitude_sine)
    return (cos_theta, sin_theta)


def combine(before_part, after_part):
    upper_left = after_part[0] * before_part[0] + after_part[1] * before_part[2]
    upper_right = after_part[0] * before_part[1] + after_part[1] * before_part[3]
    lower_left = after_part[2] * before_part[0] + after_part[3] * before_part[2]
    lower_right = after_part[2] * before_part[1] + after_part[3] * before_part[3]
    weight = jnp.abs(upper_left) + jnp.abs(upper_right) + jnp.abs(lower_left) + jnp.abs(lower_right)
    return (
        upper_left / weight,
        upper_right / weight,
        lower_left / weight,
        lower_right / weight,
        before_part[4] + after_part[4] + jnp.log(weight),
    )


def legendre_rows(m_value, cos_theta, sin_theta):
    m_float = m_value.astype(jnp.float32)
    offset_rows = jnp.arange(L, dtype=jnp.float32)[:, None]
    later_rows = jnp.maximum(offset_rows, 2.0)
    degree = m_float + later_rows
    factor = jnp.sqrt((4.0 * degree * degree - 1.0) / (later_rows * (degree + m_float)))
    damping = jnp.sqrt(
        (later_rows - 1.0)
        * (degree - 1.0 + m_float)
        / (4.0 * (degree - 1.0) * (degree - 1.0) - 1.0)
    )
    first_step = jnp.sqrt(2.0 * m_float + 3.0)
    grid_shape = (L, cos_theta.shape[0])
    upper_left = jnp.where(
        offset_rows >= 2.0,
        factor * cos_theta[None, :],
        jnp.where(offset_rows >= 1.0, first_step * cos_theta[None, :], 1.0),
    )
    upper_right = jnp.broadcast_to(
        jnp.where(offset_rows >= 2.0, -factor * damping, 0.0), grid_shape
    )
    lower_left = jnp.broadcast_to(jnp.where(offset_rows >= 1.0, 1.0, 0.0), grid_shape)
    lower_right = jnp.broadcast_to(jnp.where(offset_rows >= 1.0, 0.0, 1.0), grid_shape)
    weight = jnp.abs(upper_left) + jnp.abs(upper_right) + jnp.abs(lower_left) + jnp.abs(lower_right)
    elements = (
        upper_left / weight,
        upper_right / weight,
        lower_left / weight,
        lower_right / weight,
        jnp.log(weight),
    )
    prefix = lax.associative_scan(combine, elements, axis=0)
    log_start = 0.5 * (
        jnp.log((2.0 * m_float + 1.0) / (4.0 * math.pi))
        + lax.lgamma(m_float + 0.5)
        - 0.5 * math.log(math.pi)
        - lax.lgamma(m_float + 1.0)
    )
    log_start = log_start + m_float * jnp.log(sin_theta)[None, :]
    return prefix[0] * jnp.exp(prefix[4] + log_start)


def synthesize(harmonic_slot, m_value, cos_theta, sin_theta):
    channels = harmonic_slot.shape[0]
    flat_rows = harmonic_slot.reshape(channels * 4, L)
    padded = jnp.concatenate([flat_rows, jnp.zeros_like(flat_rows)], axis=1)
    shifted = lax.dynamic_slice_in_dim(padded, m_value, L, 1)
    legendre = legendre_rows(m_value, cos_theta, sin_theta).astype(jnp.bfloat16)
    synth_maps = jnp.dot(shifted, legendre, preferred_element_type=jnp.float32)
    return synth_maps.astype(jnp.bfloat16).reshape(channels, 2, 2, cos_theta.shape[0])


def fourier_table(m_values):
    azimuth_angle = jnp.arange(NPHI, dtype=jnp.int32)
    phase_index = m_values[:, None] * azimuth_angle[None, :] % NPHI
    angle_table = phase_index.astype(jnp.float32) * (2.0 * math.pi / NPHI)
    weight = jnp.where(m_values == 0, 1.0, 2.0)[:, None]
    return jnp.stack([weight * jnp.cos(angle_table), -weight * jnp.sin(angle_table)]).astype(
        jnp.bfloat16
    )


def synthesize_slots(spherical_harmonic, m_values, cos_theta, sin_theta):

    def one_slot(slot_pair):
        return synthesize(slot_pair[0], slot_pair[1], cos_theta, sin_theta)

    return lax.map(one_slot, (spherical_harmonic, m_values))


def local(m_table, retained_modes, cycle_ids, kl_coeffs, kl_vectors, beam_matrix):
    local_modes = kl_coeffs.shape[2]
    m_all, cycles_all = (
        lax.all_gather(m_table, "ma", axis=0, tiled=True),
        lax.all_gather(cycle_ids, "ma", axis=0, tiled=True),
    )
    offset = lax.axis_index("freq") * local_modes
    mode_index = offset + jnp.arange(local_modes, dtype=jnp.int32)
    masked = jnp.where(
        mode_index[None, None, :] < retained_modes[:, None, None],
        kl_coeffs,
        jnp.zeros_like(kl_coeffs),
    )
    summed = lax.psum_scatter(
        jnp.einsum("mqn,mnck->cmqk", masked, kl_vectors, preferred_element_type=jnp.float32),
        "freq",
        scatter_dimension=0,
        tiled=True,
    )
    singular_coefficients = summed.astype(jnp.bfloat16)
    spherical_harmonic = jnp.einsum(
        "cmqk,mclk->mcql", singular_coefficients, beam_matrix, preferred_element_type=jnp.float32
    ).astype(jnp.bfloat16)
    cos_theta, sin_theta = cycle_angles(cycles_all)
    synth_block = synthesize_slots(spherical_harmonic, m_table, cos_theta, sin_theta)
    fourier = fourier_table(m_all)
    return jnp.einsum(
        "mcsqr,qmt->rsct",
        lax.all_to_all(synth_block, "ma", split_axis=4, concat_axis=0, tiled=True),
        fourier,
        preferred_element_type=jnp.float32,
    )


def solution(mesh):
    placed = (
        P("ma"),
        P("ma"),
        P("ma"),
        P("ma", None, "freq"),
        P("ma", "freq", None, None),
        P("ma", "freq", None, None),
    )
    return jax.shard_map(
        local, mesh=mesh, in_specs=placed, out_specs=P("ma", None, "freq", None), check_vma=False
    )
```

profile of v0, /device:TPU:0, one launch (start us, length us, event | category | flops | bytes accessed | tf_op | source)
XLA Modules:
  0.0 319.3 jit_solution(416983059708512161)
XLA Ops:
  4.3 8.8 %all-reduce.98 = (s32[32]{0:T(128)S(1)}, s32[8]{0:T(128)S(1)}) all-reduce(s32[32]{0:T(128)S(1)} %dynamic-update-slice.1, s32[8]{0:T(128)S(1)} %dynamic-update-slice), channel_id=1, replica_groups=mesh['ma'=4,'freq'=8] {'ma'}, use_global_device_ids=true, to_apply=%add.96 | all-reduce | flops 40 | bytes 320
  13.9 6.7 %fusion.32 = f32[32,2,4,512]{3,2,0,1:T(4,128)S(1)} fusion(bf16[2,64,32,512]{3,2,1,0:T(8,128)(2,1)} %param.12, bf16[2,4,64]{2,1,0:T(4,128)(2,1)} %param.11, pred[2,64]{1,0:T(4,128)(4,1)S(1)} %broadcast_compare_fusion), kind=kOutput, calls=%fused_computation.238 | convolution fusion | flops 16777728 | bytes 4719744 | tf_op jit(solution)/shard_map/mqn,mnck->cmqk/dot_general | solution.py:128
  20.6 34.0 %all-reduce.100 = bf16[32,2,4,512]{3,2,0,1:T(4,128)(2,1)S(1)} all-reduce(f32[32,2,4,512]{3,2,0,1:T(4,128)S(1)} %fusion.32), channel_id=2, replica_groups=mesh['ma'=4,'freq'=8] {'freq'}, use_global_device_ids=true, to_apply=%region_0.1.clone | all-reduce | flops 131072 | bytes 786432
  55.9 5.6 %convolution_convert_fusion.1 = bf16[2,4,4,1024]{3,2,1,0:T(4,128)(2,1)S(1)} fusion(bf16[2,4,1024,512]{3,2,1,0:T(8,128)(2,1)} %param.13, bf16[32,2,4,512]{3,2,0,1:T(4,128)(2,1)S(1)} %all-reduce.100, u32[]{:T(128)S(6)} %multiply.36), kind=kOutput, calls=%fused_computation.239 | convolution fusion | flops 33587200 | bytes 8486916 | tf_op jit(solution)/shard_map/cmqk,mclk->mcql/dot_general | solution.py:134
  61.6 247.0 %while.15 = (s32[]{:T(128)}, bf16[2,4,2,2,32]{4,3,2,1,0:T(2,128)(2,1)S(1)}, bf16[2,4,4,1024]{3,2,1,0:T(4,128)(2,1)S(1)}, s32[2]{0:T(128)S(1)}, f32[32]{0:T(128)S...) while((s32[]{:T(128)}, ...), condition=%wide.region_2.3_spmd, body=%wide.region_1.2_spmd.sunk | while | flops 3591383 | bytes 16577225 | solution.py:111
  63.3 2.2 slice.3169
  65.5 2.2 slice.3170
  67.7 2.2 slice.3173
  70.0 2.2 slice.3174
  72.2 2.2 slice.3171
  74.4 2.2 slice.3172
  76.6 2.7 slice.3175
  81.6 2.2 slice.3177
  83.8 2.2 slice.3178
  158.9 2.4 slice.3301
  168.1 2.2 pad.1563
  175.0 2.4 slice.3168
  177.5 2.2 pad.1561
  188.3 2.2 slice.3170
  190.5 2.2 slice.3173
  192.8 2.2 slice.3174
  195.0 2.2 slice.3171
  197.2 2.2 slice.3172
  199.4 2.4 slice.3175
  204.0 2.2 slice.3177
  206.2 2.2 slice.3178
  281.4 2.4 slice.3301
  290.6 2.2 pad.1563
  297.4 2.6 slice.3168
  300.2 2.2 pad.1561
  309.5 3.2 %all-to-all-start = ((bf16[4,2,128]{2,1,0:T(2,128)(2,1)}), bf16[4,2,128]{2,1,0:T(2,128)(2,1)S(1)}, u32[]{:S(2)}, u32[]{:S(2)}) async-start(bf16[4,2,128]{2,1,0:T(2,128)(2,1)} %reshape.286), calls=%async_computation | async-start | bytes 4096 | tf_op jit(solution)/shard_map/all_to_all | solution.py:142
  313.0 4.2 %all-to-all-done = bf16[4,2,128]{2,1,0:T(2,128)(2,1)S(1)} async-done(((bf16[4,2,128]{2,1,0:T(2,128)(2,1)}), bf16[4,2,128]{2,1,0:T(2,128)(2,1)S(1)}, u32[]{:S(2)}, u32[]{:S(2)}) %all-to-all-start) | async-done | bytes 2080 | tf_op jit(solution)/shard_map/all_to_all | solution.py:142
  (719 shorter events, 181.9 us)
Async XLA Ops:
  0.0 54.6 %copy-start.1 = (u32[32]{0:T(128)S(1)}, u32[32]{0:T(128)}, u32[]{:S(2)}) copy-start(u32[32]{0:T(128)} %constant.572) | copy-start | bytes 388
  55.9 5.7 %copy-start = (s32[2]{0:T(128)S(1)}, s32[2]{0:T(128)}, u32[]{:S(2)}) copy-start(s32[2]{0:T(128)} %param.8) | copy-start | bytes 28
  309.5 7.8 %all-to-all-start = ((bf16[4,2,128]{2,1,0:T(2,128)(2,1)}), bf16[4,2,128]{2,1,0:T(2,128)(2,1)S(1)}, u32[]{:S(2)}, u32[]{:S(2)}) async-start(bf16[4,2,128]{2,1,0:T(2,128)(2,1)} %reshape.286), calls=%async_computation | async-start | bytes 4096 | tf_op jit(solution)/shard_map/all_to_all | solution.py:142
where the time goes:
time: 325 us; the launch traced here: 319 us
  local copies, waits for them, and re-layouts  226 us (70%)
  blocking collectives  42.8 us (13%)
  loops' own time  15.6 us (5%)
  matrix products  13.1 us (4%)
  other arithmetic  12 us (4%)
  waiting for transfers between devices  4.2 us (1%)
    slice x290, local copies, waits for them, and re-layouts, legendre_rows(): prefix = lax.associative_scan(combine, elements, axis=0)  156 us
    pad x156, local copies, waits for them, and re-layouts, legendre_rows(): prefix = lax.associative_scan(combine, elements, axis=0)  56.4 us
    unnamed x2, blocking collectives  42.8 us
    another operation x1, loops' own time, synthesize_slots(): return lax.map(one_slot, (spherical_harmonic, m_values))  15.6 us
    while x6, local copies, waits for them, and re-layouts  6.79 us
    dot_general x1, matrix products, local(): jnp.einsum('mqn,mnck->cmqk', masked, kl_vectors, preferred_element_type=j...  6.71 us
  transfers between devices with their start and end apart: 1, of which 1 were waited for; matrix products, arithmetic and copies ran while one was open for 0% of the time, Pallas kernels for 0%

commit v1 on v0

v1 whole, which is shorter than its diff:
```python
import functools
import math

import jax
import jax.numpy as jnp
from jax import lax
from jax.experimental import pallas as pl
from jax.experimental.pallas import tpu as pltpu
from jax.sharding import PartitionSpec as P

NPHI = 2048
NSIDE = 512
SEGMENTS = 8
MESH = pl.DeviceIdType.MESH
F32 = jnp.float32
BF16 = jnp.bfloat16
BIG = 2.0**30
SHRINK = 2.0**-60


def cycle_angles(cycle_numbers):
    cycle_float = cycle_numbers.astype(F32)
    nside_float = float(NSIDE)
    from_pole = jnp.minimum(cycle_float, 4.0 * nside_float - cycle_float)
    hemisphere = jnp.where(cycle_float <= 2.0 * nside_float, 1.0, -1.0)
    polar_part = from_pole * from_pole / (3.0 * nside_float * nside_float)
    polar_sin = from_pole / (math.sqrt(3.0) * nside_float) * jnp.sqrt(2.0 - polar_part)
    latitude_cosine = 4.0 / 3.0 - 2.0 * from_pole / (3.0 * nside_float)
    latitude_sine = jnp.sqrt(jnp.maximum(1.0 - latitude_cosine * latitude_cosine, 0.25))
    in_cap = from_pole < nside_float
    cos_theta = hemisphere * jnp.where(in_cap, 1.0 - polar_part, latitude_cosine)
    sin_theta = jnp.where(in_cap, polar_sin, latitude_sine)
    return (cos_theta, sin_theta)


def fourier_table(m_values):
    azimuth_angle = jnp.arange(NPHI, dtype=jnp.int32)
    phase_index = m_values[:, None] * azimuth_angle[None, :] % NPHI
    angle_table = phase_index.astype(F32) * (2.0 * math.pi / NPHI)
    weight = jnp.where(m_values == 0, 1.0, 2.0)[:, None]
    return jnp.stack([weight * jnp.cos(angle_table), -weight * jnp.sin(angle_table)]).astype(BF16)


def central_ratio(m_float):
    shifted = m_float + 0.25
    inverse = 1.0 / (shifted * shifted)
    series = 1.0 + inverse * (-1.0 / 64.0 + inverse * (21.0 / 8192.0))
    ratio = series / jnp.sqrt(math.pi * shifted)
    exact = 1.0
    for m in range(8):
        ratio = jnp.where(m_float == float(m), exact, ratio)
        exact = exact * (2 * m + 1) / (2 * m + 2)
    return ratio


def gather_kernel(
    n_ma, n_freq, m_ref, kept_ref, cyc_ref, coef_ref, vec_hbm, ints_out, svd_out,
    ints, ints_send, vec, send, recv, vec_sem, isend_sem, irecv_sem, send_sem, recv_sem,
):
    slots, quads, modes = coef_ref.shape
    channels, depth = vec_hbm.shape[2], vec_hbm.shape[3]
    n_cyc = cyc_ref.shape[0]
    rows = quads * channels
    block_rows = rows // n_freq
    ma, fr = lax.axis_index("ma"), lax.axis_index("freq")
    pieces = [
        pltpu.make_async_copy(vec_hbm.at[s], vec.at[s], vec_sem.at[s]) for s in range(slots)
    ]
    for piece in pieces:
        piece.start()
    barrier = pltpu.get_barrier_semaphore()
    for k in range(1, n_ma):
        pl.semaphore_signal(
            barrier, inc=1, device_id=(lax.rem(ma + k, n_ma), fr), device_id_type=MESH
        )
    for k in range(1, n_freq):
        pl.semaphore_signal(
            barrier, inc=1, device_id=(ma, lax.rem(fr + k, n_freq)), device_id_type=MESH
        )
    lane = lax.broadcasted_iota(jnp.int32, (8, 128), 1)
    packed = jnp.zeros((8, 128), jnp.int32)
    for i in range(n_cyc):
        packed = jnp.where(lane == i, cyc_ref[i], packed)
    for s in range(slots):
        packed = jnp.where(lane == n_cyc + s, m_ref[s], packed)
    ints_send[...] = packed
    wide = modes * channels
    row = lax.broadcasted_iota(jnp.int32, (rows, wide), 0)
    column = lax.broadcasted_iota(jnp.int32, (rows, wide), 1)
    same_channel = row // quads == column % channels
    spread = (
        lax.broadcasted_iota(jnp.int32, (modes, wide), 1) // channels
        == lax.broadcasted_iota(jnp.int32, (modes, wide), 0)
    )
    spread = jnp.where(spread, 1.0, 0.0).astype(BF16)
    repeat = (
        lax.broadcasted_iota(jnp.int32, (rows, quads), 0) % quads
        == lax.broadcasted_iota(jnp.int32, (rows, quads), 1)
    )
    repeat = jnp.where(repeat, 1.0, 0.0).astype(BF16)
    mode = fr * modes + lax.broadcasted_iota(jnp.int32, (quads, modes), 1)
    pl.semaphore_wait(barrier, n_ma - 1 + n_freq - 1)
    int_copies = []
    for k in range(1, n_ma):
        copy = pltpu.make_async_remote_copy(
            src_ref=ints_send, dst_ref=ints.at[k], send_sem=isend_sem.at[k],
            recv_sem=irecv_sem.at[k], device_id=(lax.rem(ma + k, n_ma), fr), device_id_type=MESH,
        )
        copy.start()
        int_copies.append(copy)
    for s in range(slots):
        masked = jnp.where(mode < kept_ref[s], coef_ref[s].astype(F32), 0.0).astype(BF16)
        tall = jnp.dot(repeat, masked, preferred_element_type=F32).astype(BF16)
        full = jnp.dot(tall, spread, preferred_element_type=F32)
        weights = jnp.where(same_channel, full, 0.0).astype(BF16)
        pieces[s].wait()
        flat = vec[s].reshape(wide, depth)
        part = jnp.dot(weights, flat, preferred_element_type=F32).astype(BF16)
        for f in range(n_freq):
            send[f, s] = part[f * block_rows : (f + 1) * block_rows]
    copies = []
    for k in range(1, n_freq):
        to = lax.rem(fr + k, n_freq)
        copy = pltpu.make_async_remote_copy(
            src_ref=send.at[to], dst_ref=recv.at[k], send_sem=send_sem.at[k],
            recv_sem=recv_sem.at[k], device_id=(ma, to), device_id_type=MESH,
        )
        copy.start()
        copies.append(copy)
    for copy in int_copies:
        copy.wait()
    ints_out[0] = packed
    for k in range(1, n_ma):
        ints_out[k] = ints[k]
    total = send[fr].astype(F32)
    for k in range(1, n_freq):
        copies[k - 1].wait()
        total = total + recv[k].astype(F32)
    svd_out[...] = total.astype(BF16)


def gather_call(n_ma, n_freq, m_table, retained_modes, cycle_ids, kl_coeffs, kl_vectors):
    slots, quads, modes = kl_coeffs.shape
    channels, depth = kl_vectors.shape[2:]
    block_rows = quads * channels // n_freq
    smem = pl.BlockSpec(memory_space=pltpu.SMEM)
    vmem = pl.BlockSpec(memory_space=pltpu.VMEM)
    return pl.pallas_call(
        functools.partial(gather_kernel, n_ma, n_freq),
        out_shape=(
            jax.ShapeDtypeStruct((n_ma, 8, 128), jnp.int32),
            jax.ShapeDtypeStruct((slots, block_rows, depth), BF16),
        ),
        in_specs=[smem, smem, smem, vmem, pl.BlockSpec(memory_space=pl.ANY)],
        out_specs=(vmem, vmem),
        scratch_shapes=[
            pltpu.VMEM((n_ma, 8, 128), jnp.int32),
            pltpu.VMEM((8, 128), jnp.int32),
            pltpu.VMEM(kl_vectors.shape, BF16),
            pltpu.VMEM((n_freq, slots, block_rows, depth), BF16),
            pltpu.VMEM((n_freq, slots, block_rows, depth), BF16),
            pltpu.SemaphoreType.DMA((slots,)),
            pltpu.SemaphoreType.DMA((n_ma,)),
            pltpu.SemaphoreType.DMA((n_ma,)),
            pltpu.SemaphoreType.DMA((n_freq,)),
            pltpu.SemaphoreType.DMA((n_freq,)),
        ],
        compiler_params=pltpu.CompilerParams(collective_id=0, has_side_effects=True),
        name="gather_svd",
    )(m_table, retained_modes, cycle_ids, kl_coeffs, kl_vectors)


def legendre_into(par_ref, rows_ref, exps_ref, leg_ref):
    length, _, wide = rows_ref.shape
    half = wide // 2
    shape = (SEGMENTS, wide)
    m = jnp.broadcast_to(par_ref[0:1, :], shape)
    c = jnp.broadcast_to(par_ref[1:2, :], shape)
    first = lax.broadcasted_iota(jnp.int32, shape, 1) < half
    base = (lax.broadcasted_iota(jnp.int32, shape, 0) * length).astype(F32)

    def ratio(degree):
        after = degree - m > 0.5
        y = (degree - m) * (degree + m) / ((2.0 * degree - 1.0) * (2.0 * degree + 1.0))
        y = jnp.where(after, y, 1.0)
        a = lax.rsqrt(y)
        a = a * (1.5 - 0.5 * y * a * a)
        return (after, a, jnp.where(after, y * a, 0.0))

    steps = 4

    def body(i, state):
        p1, p2, e, root = state
        for u in range(steps):
            j = i * steps + u
            after, a, next_root = ratio(base + j.astype(F32))
            p = jnp.where(after, a * c, 1.0) * p1 - a * root * p2
            p1, p2, root = p, p1, next_root
            rows_ref[j] = p
            exps_ref[j] = e
        large = jnp.maximum(jnp.abs(p1), jnp.abs(p2)) > BIG
        scale = jnp.where(large, SHRINK, 1.0)
        return (p1 * scale, p2 * scale, jnp.where(large, e + 60.0, e), root)

    one = jnp.where(first, 1.0, 0.0)
    lax.fori_loop(
        0, length // steps, body,
        (one, 1.0 - one, jnp.zeros(shape, F32), ratio(base - 1.0)[2]), unroll=2,
    )
    last, last_e = rows_ref[length - 1], exps_ref[length - 1]
    before, before_e = rows_ref[length - 2], exps_ref[length - 2]
    top = jnp.maximum(last_e, pltpu.roll(last_e, half, 1))
    last = last * jnp.exp2(jnp.maximum(last_e - top, -126.0))
    before = before * jnp.exp2(jnp.maximum(before_e - top, -126.0))
    x = jnp.where(first[0:1], par_ref[2:3, :], 0.0)
    x_e = par_ref[3:4, :]
    starts, starts_e = [], []
    for s in range(SEGMENTS):
        starts.append(x)
        starts_e.append(x_e)
        if s < SEGMENTS - 1:
            t1, t2 = x * last[s : s + 1], x * before[s : s + 1]
            t1, t2 = t1 + pltpu.roll(t1, half, 1), t2 + pltpu.roll(t2, half, 1)
            size = jnp.maximum(jnp.abs(t1), jnp.abs(t2))
            x = jnp.where(first[0:1], t1, t2)
            large, small = size > BIG, size < 1.0 / BIG
            x = x * jnp.where(large, SHRINK, jnp.where(small, 1.0 / SHRINK, 1.0))
            x_e = x_e + top[s : s + 1] + jnp.where(large, 60.0, jnp.where(small, -60.0, 0.0))
    for s in range(SEGMENTS):
        exponent = exps_ref[:, s, :] + starts_e[s]
        low = jnp.floor(exponent * 0.5)
        degree = (
            s * length + lax.broadcasted_iota(jnp.int32, (length, wide), 0)
        ).astype(F32)
        value = rows_ref[:, s, :] * jnp.exp2(jnp.maximum(low, -126.0)) * starts[s]
        value = value * jnp.exp2(jnp.maximum(exponent - low, -126.0))
        value = jnp.where(degree >= par_ref[0:1, :], value, 0.0)
        turned = value.T
        leg_ref[:, s * length : (s + 1) * length] = (turned[:half] + turned[half:]).astype(BF16)


def synth_kernel(par_ref, svd_ref, beam_ref, out_ref, rows_ref, exps_ref, leg_ref):
    s, c = pl.program_id(0), pl.program_id(1)
    slots, block_rows, depth = svd_ref.shape
    n_ch = pl.num_programs(1)
    cycles = leg_ref.shape[0] // slots
    quads = 4

    @pl.when((s == 0) & (c == 0))
    def _():
        legendre_into(par_ref, rows_ref, exps_ref, leg_ref)
        out_ref[...] = jnp.zeros_like(out_ref)

    leg = leg_ref[pl.ds(pl.multiple_of(s * cycles, cycles), cycles), :]
    table = jnp.dot(leg, beam_ref[0, 0], preferred_element_type=F32).astype(BF16)
    svd = svd_ref[...].reshape(slots * block_rows, depth)
    svd = jnp.concatenate([svd, jnp.zeros((128 - slots * block_rows, depth), BF16)], axis=0)
    modes = lax.dot_general(
        table, svd, (((1,), (1,)), ((), ())), preferred_element_type=F32
    )
    group = lax.broadcasted_iota(jnp.int32, modes.shape, 1) // quads
    out_ref[...] += jnp.where(group == s * n_ch + c, modes, 0.0)


def synth_call(params, svd, beam_matrix, cycles):
    slots, channels, length, depth = beam_matrix.shape
    wide = params.shape[1]
    return pl.pallas_call(
        synth_kernel,
        grid=(slots, channels),
        out_shape=jax.ShapeDtypeStruct((cycles, 128), F32),
        in_specs=[
            pl.BlockSpec(params.shape, lambda s, c: (0, 0)),
            pl.BlockSpec(svd.shape, lambda s, c: (0, 0, 0)),
            pl.BlockSpec((1, 1, length, depth), lambda s, c: (s, c, 0, 0)),
        ],
        out_specs=pl.BlockSpec((cycles, 128), lambda s, c: (0, 0)),
        scratch_shapes=[
            pltpu.VMEM((length // SEGMENTS, SEGMENTS, wide), F32),
            pltpu.VMEM((length // SEGMENTS, SEGMENTS, wide), F32),
            pltpu.VMEM((slots * cycles, length), BF16),
        ],
        name="synth_cycles",
    )(params, svd, beam_matrix)


def swap_kernel(n_ma, in_ref, out_ref, recv, send_sem, recv_sem):
    ma, fr = lax.axis_index("ma"), lax.axis_index("freq")
    mine = recv.shape[1]
    barrier = pltpu.get_barrier_semaphore()
    for k in range(1, n_ma):
        pl.semaphore_signal(
            barrier, inc=1, device_id=(lax.rem(ma + k, n_ma), fr), device_id_type=MESH
        )
    pl.semaphore_wait(barrier, n_ma - 1)
    copies = []
    for k in range(1, n_ma):
        to = lax.rem(ma + k, n_ma)
        copy = pltpu.make_async_remote_copy(
            src_ref=in_ref.at[pl.ds(pl.multiple_of(to * mine, mine), mine)],
            dst_ref=recv.at[k], send_sem=send_sem.at[k], recv_sem=recv_sem.at[k],
            device_id=(to, fr), device_id_type=MESH,
        )
        copy.start()
        copies.append(copy)
    out_ref[0] = in_ref[pl.ds(pl.multiple_of(ma * mine, mine), mine)]
    for k in range(1, n_ma):
        copies[k - 1].wait()
        out_ref[k] = recv[k]


def swap_call(n_ma, modes):
    mine = modes.shape[0] // n_ma
    vmem = pl.BlockSpec(memory_space=pltpu.VMEM)
    return pl.pallas_call(
        functools.partial(swap_kernel, n_ma),
        out_shape=jax.ShapeDtypeStruct((n_ma, mine, 128), F32),
        in_specs=[vmem],
        out_specs=vmem,
        scratch_shapes=[
            pltpu.VMEM((n_ma, mine, 128), F32),
            pltpu.SemaphoreType.DMA((n_ma,)),
            pltpu.SemaphoreType.DMA((n_ma,)),
        ],
        compiler_params=pltpu.CompilerParams(collective_id=1, has_side_effects=True),
        name="swap_cycles",
    )(modes)


def local(n_ma, n_freq, m_table, retained_modes, cycle_ids, kl_coeffs, kl_vectors, beam_matrix):
    slots, n_cyc = m_table.shape[0], cycle_ids.shape[0]
    channels, length = beam_matrix.shape[1:3]
    cycles = n_cyc * n_ma
    ints, svd = gather_call(
        n_ma, n_freq, m_table, retained_modes, cycle_ids, kl_coeffs, kl_vectors
    )
    ma = lax.axis_index("ma")
    numbers = ints[:, 0, :]
    source = lax.rem(ma - jnp.arange(n_ma) + n_ma, n_ma)
    cos_theta, sin_theta = cycle_angles(
        numbers[:, :n_cyc].reshape(cycles)
    )
    m_float = m_table.astype(F32)[:, None]
    mantissa = jnp.sqrt((2.0 * m_float + 1.0) / (4.0 * math.pi) * central_ratio(m_float))
    power = m_float * (jnp.log(sin_theta) * (1.0 / math.log(2.0)))[None, :]
    whole = jnp.floor(power)
    mantissa = mantissa * jnp.exp2(power - whole)
    both = lambda a: jnp.tile(jnp.broadcast_to(a, (slots, cycles)).reshape(1, -1), (1, 2))
    params = jnp.concatenate(
        [both(m_float), both(cos_theta[None, :]), both(mantissa), both(whole)]
        + [jnp.zeros((4, 2 * slots * cycles), F32)], axis=0
    )
    modes = synth_call(params, svd, beam_matrix, cycles)
    modes = modes.reshape(n_ma, n_cyc, 128)[source].reshape(cycles, 128)
    swapped = swap_call(n_ma, modes)[:, :, : slots * channels * 4]
    swapped = swapped.reshape(n_ma, n_cyc, slots, channels, 2, 2).astype(BF16)
    fourier = fourier_table(numbers[:, n_cyc : n_cyc + slots].reshape(n_ma * slots))
    fourier = fourier.reshape(2, n_ma, slots, NPHI)
    return jnp.einsum("arscde,east->rdct", swapped, fourier, preferred_element_type=F32)


def solution(mesh):
    placed = (
        P("ma"),
        P("ma"),
        P("ma"),
        P("ma", None, "freq"),
        P("ma", "freq", None, None),
        P("ma", "freq", None, None),
    )
    return jax.shard_map(
        functools.partial(local, mesh.shape["ma"], mesh.shape["freq"]),
        mesh=mesh, in_specs=placed, out_specs=P("ma", None, "freq", None), check_vma=False,
    )
```

time: 325 us -> 39.5 us (0.12); the launches traced: 319 us -> 38.9 us
  local copies, waits for them, and re-layouts: 226 us -> 6.42 us
  blocking collectives: 42.8 us -> 0 us
  Pallas kernels: 0 us -> 30.1 us
  loops' own time: 15.6 us -> 0 us
  matrix products: 13.1 us -> 0.27 us
  other arithmetic: 12 us -> 2.08 us
  waiting for transfers between devices: 4.2 us -> 0 us
    slice x290 -> x5, local copies, waits for them, and re-layouts: 156 us -> 1.7 us  [the longest x2 0.82 us: local(): swapped = swap_call(n_ma, modes)[:, :, :slots * channels * 4]]
    pad x156 -> x0, local copies, waits for them, and re-layouts: 56.4 us -> none  [legendre_rows(): prefix = lax.associative_scan(combine, elements, axis=0)]
    unnamed x2 -> x0, blocking collectives: 42.8 us -> none
    pallas_call x0 -> x3, Pallas kernels: none -> 30.1 us  [the longest x1 14.6 us: gather_call(): pl.pallas_call(functools.partial(gather_kernel, n_ma, n_freq), out_shape=...]
    another operation x1 -> x0, loops' own time: 15.6 us -> none  [synthesize_slots(): return lax.map(one_slot, (spherical_harmonic, m_values))]
    dot_general x5 -> x1, matrix products: 13.1 us -> 0.27 us  [local(): jnp.einsum('arscde,east->rdct', swapped, fourier, preferred_element_type=...]
    while x7 -> x0, local copies, waits for them, and re-layouts: 6.93 us -> none
    concatenate x84 -> x0, other arithmetic: 6.47 us -> none  [legendre_rows(): prefix = lax.associative_scan(combine, elements, axis=0)]
  transfers between devices with their start and end apart: 1 -> 0, of which waited for: 1 -> 0; matrix products, arithmetic and copies ran while one was open for 0% -> 0% of each run, Pallas kernels for 0% -> 0%
where the time goes in v1:
time: 39.5 us; the launch traced here: 38.9 us
  Pallas kernels  30.1 us (76%)
  local copies, waits for them, and re-layouts  6.42 us (16%)
  other arithmetic  2.08 us (5%)
    pallas_call x1, Pallas kernels, gather_call(): pl.pallas_call(functools.partial(gather_kernel, n_ma, n_freq), out_shape=...  14.6 us
    pallas_call x1, Pallas kernels, synth_call(): pl.pallas_call(synth_kernel, grid=(slots, channels), out_shape=jax.ShapeD...  9.57 us
    pallas_call x1, Pallas kernels, swap_call(): pl.pallas_call(functools.partial(swap_kernel, n_ma), out_shape=jax.ShapeD...  5.9 us
    gather x1, local copies, waits for them, and re-layouts, local(): modes = modes.reshape(n_ma, n_cyc, 128)[source].reshape(cycles, 128)  1.86 us
    transpose x1, local copies, waits for them, and re-layouts, local(): jnp.einsum('arscde,east->rdct', swapped, fourier, preferred_element_type=...  1.13 us
    slice x2, local copies, waits for them, and re-layouts, local(): swapped = swap_call(n_ma, modes)[:, :, :slots * channels * 4]  0.82 us

profile of v1, /device:TPU:0, one launch (start us, length us, event | category | flops | bytes accessed | tf_op | source)
XLA Modules:
  0.0 38.9 jit_solution(5237874050728360824)
XLA Ops:
  0.0 0.7 %fusion.11 = f32[2]{0:T(128)S(1)} fusion(s32[2]{0:T(128)} %m_ref.1), kind=kLoop, calls=%fused_computation.39 | loop fusion | flops 60 | bytes 16 | tf_op jit(solution)/shard_map/sqrt | solution.py:344
  0.7 0.1 mul.196
  0.8 0.1 mul.197
  0.8 0.7 %convert_element_type.39 = f32[2]{0:T(128)S(1)} convert(s32[2]{0:T(128)} %m_ref.1) | non-fusion elementwise | flops 2 | bytes 16 | tf_op jit(solution)/shard_map/convert_element_type | solution.py:343
  1.5 0.1 broadcast_in_dim.60
  1.6 0.1 tile.36
  1.7 0.1 tile.38
  1.8 14.6 %gather_svd.1 = (s32[4,8,128]{2,1,0:T(8,128)}, bf16[2,16,512]{2,1,0:T(8,128)(2,1)}) custom-call(s32[2]{0:T(128)} %m_ref.1, s32[2]{0:T(128)} %kept_ref.1, s32[8]{0:T(128)} %cyc_ref.1, bf16[2,4,64]{2,1,0:T(4,128)(2,1)} %coef_ref.1, bf16[2,64,32,512]{3,2,1,0:T(8,128)(2,1)} %vec_hbm.1), custom_call_target="tpu_custom_call" | custom-call | tf_op jit(solution)/shard_map/gather_svd/pallas_call | solution.py:148
  16.4 0.7 %slice.13 = s32[4,1,128]{2,1,0:T(1,128)S(1)} slice(s32[4,8,128]{2,1,0:T(8,128)} %get-tuple-element.7), slice={[0:4], [0:1], [0:128]} | slice | bytes 4096 | tf_op jit(solution)/shard_map/slice | solution.py:338
  17.1 0.1 convert_element_type.41
  17.3 0.1 mul.203
  17.4 0.1 tile.45
  17.4 0.1 tile.43
  17.5 0.1 tile.39
  17.6 0.1 tile.41
  17.7 0.6 %concatenate.5.par_ref = f32[8,128]{1,0:T(8,128)} concatenate(f32[1,128]{1,0:T(1,128)S(1)} %tile.38, f32[1,128]{1,0:T(1,128)S(1)} %tile.41, f32[1,128]{1,0:T(1,128)S(1)} %tile.43, f32[1,128]{1,0:T(1,128)S(1)} %tile.45, f32[4,128]{1,0:T(4,128)S(1)} %broadcast_in_dim.71), dimensions={0} | concatenate | bytes 8192 | tf_op jit(solution)/shard_map/concatenate | solution.py:349
  18.3 9.6 %synth_cycles.1 = f32[32,128]{1,0:T(8,128)} custom-call(f32[8,128]{1,0:T(8,128)} %concatenate.5.par_ref, bf16[2,16,512]{2,1,0:T(8,128)(2,1)} %get-tuple-element.8.svd_ref, bf16[2,4,1024,512]{3,2,1,0:T(8,128)(2,1)} %beam_ref.1), custom_call_target="tpu_custom_call" | custom-call | tf_op jit(solution)/shard_map/synth_cycles/pallas_call | solution.py:268
  27.9 1.9 %gather_fusion = f32[4,8,128]{2,1,0:T(8,128)} fusion(f32[4,8,128]{2,1,0:T(8,128)} %bitcast.18, s32[1024]{0:T(1024)S(1)} %pad_clamp_fusion), kind=kCustom, calls=%fused_computation | custom fusion | bytes 32784 | tf_op jit(solution)/shard_map/gather | solution.py:354
  29.8 5.9 %swap_cycles.1 = f32[4,8,128]{2,1,0:T(8,128)} custom-call(f32[32,128]{1,0:T(8,128)} %bitcast.19), custom_call_target="tpu_custom_call" | custom-call | tf_op jit(solution)/shard_map/swap_cycles/pallas_call | solution.py:315
  35.7 0.7 %slice.25 = bf16[4,8,32]{2,1,0:T(8,128)(2,1)S(1)} slice(f32[4,8,128]{2,1,0:T(8,128)} %swap_cycles.1), slice={[0:4], [0:8], [0:32]} | slice | bytes 4096 | tf_op jit(solution)/shard_map/slice | solution.py:355
  36.4 0.1 slice.14
  36.5 0.1 copy.13
  36.6 0.1 compare_select_fusion.12
  36.6 0.1 copy.12
  36.7 0.1 copy.14
  36.8 0.1 copy.15
  36.9 0.6 %multiply_convert_fusion.1 = (bf16[1,4,2,2048]{3,1,2,0:T(4,128)(2,1)S(1)}, bf16[1,4,2,2048]{3,1,2,0:T(4,128)(2,1)S(1)}) fusion(s32[4,2]{0,1:T(2,128)S(1)} %copy.13, f32[4,2]{0,1:T(2,128)S(1)} %copy.12, f32[4,2]{0,1:T(2,128)S(1)} %copy.14), kind=kLoop, calls=%fused_computation.12 | loop fusion | flops 294912 | bytes 65632 | tf_op jit(solution)/shard_map/convert.1
  37.5 0.3 convolution_bitcast_fusion
  37.8 1.1 %copy.17 = f32[8,2,4,2048]{3,2,1,0:T(4,128)} copy(f32[8,2,4,2048]{3,0,1,2:T(8,128)S(1)} %convolution_bitcast_fusion) | data formatting | bytes 1048576 | tf_op jit(solution)/shard_map/arscde,east->rdct/transpose | solution.py:359
  (12 shorter events, 0.1 us)
